TPU v7x, 32 devices: a whole 2x2x4 slice. The times are simulated.
32 devices in a mesh: view: 4 (over y, core), slab: 8 (over z, x).
Axes of the slice: x: 2, y: 2, z: 4, core: 2. Of those that a mesh axis runs over, the one named last changes fastest.
Arguments:
- estimate: float32 [2, 128, 128, 1024], P(None, 'slab', 'view'), may hold values from 0.2 to 5
- recorded: bfloat16 [2, 2, 128, 128, 1024], P(None, None, None, 'view', 'slab'), may hold values from 0.19921875 to 5
- psf_lateral: float32 [2, 2, 31], replicated, may hold values from 0.0007 to 1.5, as said below
- psf_axial: float32 [2, 127], replicated, may hold values from 0.0007 to 1.5, as said below
- offsets: int32 [2, 2], replicated, may hold values from -8 to 8, as said below
Outputs:
- updated: float32 [2, 128, 128, 1024], P(None, 'slab', 'view')
Inputs may be any that keep to these rules, and one draw needn't show every extreme that they name: offsets[v] is imaging direction v's voxel shift along x and along y; the magnitude 8 occurs with both signs. `psf_lateral`: positive lateral taps. `psf_axial`: positive axial taps.
All inputs are finite; a program needn't handle non-finite values.
Results may differ from a plain program's by a relative error of at most 0.0003.
Values sent between devices are 32-bit elements; how exact they have to be, the bound alone decides.
No kernel may reach another device: no remote copies, remote signals or barrier semaphores. Data moves between devices by JAX's collectives and lax.ppermute only.
A program may use at most 128 MiB of HBM per device.

v0:
```python
import jax
import jax.numpy as jnp
from jax import lax
from jax.sharding import PartitionSpec as P

Z = 128
YBLK = 128
HALO = 23
BACKGROUND = 0.05
HIGHEST = lax.Precision.HIGHEST


def with_halo(value, sides, width):
    for axis, dim in sides:
        peers, length = (lax.axis_size(axis), value.shape[dim])
        up = [(i, (i + 1) % peers) for i in range(peers - 1)]
        down = [(j, i) for i, j in up]
        last = lax.slice_in_dim(value, length - width, length, axis=dim)
        leading = lax.slice_in_dim(value, 0, width, axis=dim)
        before = lax.ppermute(last, axis, up)
        after = lax.ppermute(leading, axis, down)
        value = jnp.concatenate([before, value, after], axis=dim)
    return value


def unit_taps(weights):
    return weights / jnp.sum(weights)


def band_table(weights, places):
    levels = jnp.arange(weights.shape[0], dtype=jnp.int32)
    return jnp.sum(jnp.where(places[..., None] == levels, weights, 0.0), axis=-1)


def margin_matrix(weights, offset, length, margin, adjoint):
    centre = (weights.shape[0] - 1) // 2
    outputs = jnp.arange(length, dtype=jnp.int32)[:, None]
    sources = jnp.arange(length + 2 * margin, dtype=jnp.int32)[None, :] - margin
    apart = sources - outputs
    if adjoint:
        apart = -apart
    return band_table(weights, apart - offset + centre)


def blocked_rows(field, weights, offset, width_blk, adjoint):
    extent = field.shape
    blocks = extent[3] // width_blk
    pieces = field.reshape(extent[0], extent[1], extent[2], blocks, width_blk)
    padded = jnp.pad(pieces, ((0, 0), (0, 0), (0, 0), (1, 1), (0, 0)))
    centre = (weights.shape[0] - 1) // 2
    sources = jnp.arange(width_blk, dtype=jnp.int32)[:, None]
    outputs = jnp.arange(width_blk, dtype=jnp.int32)[None, :]
    result = jnp.zeros(pieces.shape, jnp.float32)
    for shifted in range(3):
        apart = (shifted - 1) * width_blk + sources - outputs
        if adjoint:
            apart = -apart
        matrix = band_table(weights, apart - offset + centre)
        result = result + jnp.einsum(
            "czxkj,ji->czxki",
            padded[:, :, :, shifted : shifted + blocks],
            matrix,
            precision=HIGHEST,
        )
    return result.reshape(extent)


def shards(estimate, recorded, psf_lateral, psf_axial, offsets):
    views_n = recorded.shape[0]
    along_x = [unit_taps(psf_lateral[which, 0]) for which in range(views_n)]
    along_y = [unit_taps(psf_lateral[which, 1]) for which in range(views_n)]
    rows_at = jnp.arange(Z, dtype=jnp.int32)[:, None]
    cols_at = jnp.arange(Z, dtype=jnp.int32)[None, :]
    axial_places = cols_at - rows_at + (psf_axial.shape[1] - 1) // 2
    axial = [band_table(unit_taps(psf_axial[which]), axial_places) for which in range(views_n)]
    x_rows = estimate.shape[2]
    widened = with_halo(estimate, (("view", 2),), HALO)
    blurred = []
    for which in range(views_n):
        across = margin_matrix(along_x[which], offsets[which, 0], x_rows, HALO, False)
        sectioned = jnp.einsum("ab,czby->czay", across, widened, precision=HIGHEST)
        blurred.append(blocked_rows(sectioned, along_y[which], offsets[which, 1], YBLK, False))
    columns = lax.all_to_all(jnp.stack(blurred), "slab", split_axis=4, concat_axis=2, tiled=True)
    spread = []
    for which in range(views_n):
        imaged = jnp.einsum("oi,cixy->coxy", axial[which], columns[which], precision=HIGHEST)
        quotient = recorded[which].astype(jnp.float32) / (imaged + BACKGROUND)
        spread.append(jnp.einsum("oi,coxy->cixy", axial[which], quotient, precision=HIGHEST))
    planes = lax.all_to_all(jnp.stack(spread), "slab", split_axis=2, concat_axis=4, tiled=True)
    returned = [
        blocked_rows(planes[which], along_y[which], offsets[which, 1], YBLK, True)
        for which in range(views_n)
    ]
    fringe = with_halo(jnp.stack(returned), (("view", 3),), HALO)
    summed = jnp.zeros(estimate.shape, jnp.float32)
    for which in range(views_n):
        across = margin_matrix(along_x[which], offsets[which, 0], x_rows, HALO, True)
        summed = summed + jnp.einsum("ab,czby->czay", across, fringe[which], precision=HIGHEST)
    return estimate * (summed / views_n)


def solution(mesh):
    in_specs = (P(None, "slab", "view", None), P(None, None, None, "view", "slab"), P(), P(), P())
    out_specs = P(None, "slab", "view", None)
    return jax.shard_map(shards, mesh=mesh, in_specs=in_specs, out_specs=out_specs, check_vma=False)
```

profile of v0, /device:TPU:1, one launch (start us, length us, event | category | flops | bytes accessed | tf_op | source)
XLA Modules:
  0.0 831.5 jit_solution(896550517628313579)
XLA Ops:
  30.3 12.5 %collective-permute-done = f32[2,16,23,1024]{3,1,2,0:T(8,128)S(1)} collective-permute-done((f32[2,16,23,1024]{3,1,2,0:T(8,128)S(1)}, f32[2,16,23,1024]{3,1,2,0:T(8,128)S(1)}, u32[]{:S(2)}, u32[]{:S(2)}) %collective-permute-start) | collective-permute-done | bytes 3014688 | tf_op jit(solution)/shard_map/ppermute | solution.py:20
  50.7 11.1 %fusion.3 = f32[2,16,1024,32]{2,3,1,0:T(8,128)S(1)} fusion(f32[2,16,23,1024]{3,2,1,0:T(8,128)S(1)} %copy.64, f32[2,16,32,1024]{3,2,1,0:T(8,128)S(1)} %copy-done, f32[2,16,23,1024]{3,2,1,0:T(8,128)S(1)} %copy.63, f32[32,78]{1,0:T(8,128)S(1)} %get-tuple-element.61), kind=kOutput, calls=%fused_computation.21 | convolution fusion | flops 986578944 | bytes 14427904 | tf_op jit(solution)/shard_map/ab,czby->czay/dot_general | solution.py:81
  79.9 13.7 %fusion.2 = f32[2,16,1024,32]{2,3,1,0:T(8,128)S(1)} fusion(f32[2,16,23,1024]{3,2,1,0:T(8,128)} %copy-done.4, f32[2,16,32,1024]{3,2,1,0:T(8,128)} %param.5, f32[2,16,23,1024]{3,2,1,0:T(8,128)S(1)} %copy.63, f32[32,78]{1,0:T(8,128)S(1)} %get-tuple-element.16), kind=kOutput, calls=%fused_computation.20 | convolution fusion | flops 986578944 | bytes 14427904 | tf_op jit(solution)/shard_map/ab,czby->czay/dot_general | solution.py:81
  111.2 8.3 %pad_maximum_fusion.2 = f32[2,2,16,32,1024]{4,3,2,1,0:T(8,128)} fusion(f32[1,2,16,32,1024]{4,3,2,1,0:T(8,128)} %stack_reshape.13, f32[1,2,16,32,1024]{4,3,2,1,0:T(8,128)} %stack_reshape.12), kind=kLoop, calls=%fused_computation.14 | loop fusion | flops 2097152 | bytes 16777216 | tf_op jit(solution)/shard_map/stack | solution.py:83
  119.6 26.6 %copy.65 = f32[2,2,16,32,1024]{3,2,1,0,4:T(8,128)} copy(f32[2,2,16,32,1024]{4,3,2,1,0:T(8,128)} %pad_maximum_fusion.2) | data formatting | bytes 16777216 | tf_op jit(solution)/shard_map/stack | solution.py:83
  146.1 20.5 %reshape.373 = f32[8,1,262144]{2,1,0:T(1,128)} reshape(f32[1024,2,2,16,32]{4,3,2,1,0:T(8,128)} %bitcast.192) | data formatting | bytes 16777216
  166.6 5.5 all-to-all-start
  187.9 150.7 %all-to-all-done = f32[8,1,262144]{2,1,0:T(1,128)} async-done(((f32[8,1,262144]{2,1,0:T(1,128)}), f32[8,1,262144]{2,1,0:T(1,128)}, u32[]{:S(2)}, u32[]{:S(2)}) %all-to-all-start) | async-done | bytes 8388640 | tf_op jit(solution)/shard_map/all_to_all | solution.py:83
  339.1 26.4 %reduce.6 = f32[8,262144]{1,0:T(8,128)} reduce(f32[8,1,262144]{2,1,0:T(1,128)} %all-to-all-done, f32[]{:T(128)} %broadcast.385), dimensions={1}, to_apply=%all_to_all.22.reduce_sub_computation | reduce | bytes 16777220 | tf_op jit(solution)/shard_map/all_to_all | solution.py:83
  365.5 25.3 %reshape.374 = f32[1024,2,2,16,32]{4,3,2,1,0:T(8,128)} reshape(f32[8,262144]{1,0:T(8,128)} %reduce.6) | data formatting | bytes 16777216
  390.7 18.4 %copy.97 = f32[2,2,16,32,8,128]{5,4,3,2,1,0:T(8,128)} copy(f32[2,2,16,32,8,128]{3,2,1,0,5,4:T(8,128)} %bitcast.193) | data formatting | bytes 16777216 | tf_op jit(solution)/shard_map/all_to_all | solution.py:83
  414.8 8.4 %fusion.18 = f32[2,32,128,128]{3,2,1,0:T(8,128)S(1)} fusion(f32[2,128,32,128]{3,2,1,0:T(8,128)S(1)} %bitcast.206, f32[128,128]{1,0:T(8,128)S(1)} %get-tuple-element.5), kind=kOutput, calls=%fused_computation.41 | convolution fusion | flops 1610612736 | bytes 8454144 | tf_op jit(solution)/shard_map/oi,cixy->coxy/dot_general | solution.py:86
  427.3 8.4 %fusion.16 = f32[2,32,128,128]{3,2,1,0:T(8,128)S(1)} fusion(f32[2,128,32,128]{3,2,1,0:T(8,128)S(1)} %bitcast.205, f32[128,128]{1,0:T(8,128)S(1)} %get-tuple-element.6), kind=kOutput, calls=%fused_computation.39 | convolution fusion | flops 1610612736 | bytes 8454144 | tf_op jit(solution)/shard_map/oi,cixy->coxy/dot_general | solution.py:86
  443.8 10.3 %copy.72 = f32[2,2,128,32,128]{4,3,1,0,2:T(8,128)} copy(f32[2,2,128,32,128]{2,4,3,1,0:T(8,128)} %pad_maximum_fusion.3) | data formatting | bytes 16777216 | tf_op jit(solution)/shard_map/stack | solution.py:89
  454.1 187.0 %all_to_all.30 = f32[2,2,128,32,128]{4,3,1,0,2:T(8,128)S(1)} all-to-all(f32[2,2,128,32,128]{4,3,1,0,2:T(8,128)} %copy.72), channel_id=1, replica_groups=mesh['view'=4,'slab'=8] {'slab'}, dimensions={2} | all-to-all | bytes 16777216 | tf_op jit(solution)/shard_map/all_to_all | solution.py:89
  641.1 8.1 copy.111
  670.6 5.3 fusion.33
  696.6 9.5 %fusion.68 = (f32[2,2,16,23,1024]{4,3,2,1,0:T(8,128)}, f32[2,2,16,23,1024]{4,3,2,1,0:T(8,128)S(1)}) fusion(f32[2,2,16,32,1024]{4,3,2,1,0:T(8,128)} %constant_dynamic-update-slice_fusion), kind=kLoop, calls=%fused_computation.165 | loop fusion | bytes 24117248 | tf_op jit(solution)/shard_map/slice | solution.py:18
  706.2 6.3 copy.75
  721.8 59.3 %collective-permute-done.2 = f32[2,2,16,23,1024]{4,2,3,1,0:T(8,128)S(1)} collective-permute-done((f32[2,2,16,23,1024]{4,2,3,1,0:T(8,128)S(1)}, f32[2,2,16,23,1024]{4,2,3,1,0:T(8,128)S(1)}, u32[]{:S(2)}, u32[]{:S(2)}) %collective-permute-start.2) | collective-permute-done | bytes 6029344 | tf_op jit(solution)/shard_map/ppermute | solution.py:20
  789.4 6.2 copy.78
  795.6 8.4 %pad_maximum_fusion = f32[2,2,16,78,1024]{4,3,2,1,0:T(8,128)S(1)} fusion(f32[2,2,16,23,1024]{4,3,2,1,0:T(8,128)} %copy.78, f32[2,2,16,32,1024]{4,3,2,1,0:T(8,128)} %constant_dynamic-update-slice_fusion, f32[2,2,16,23,1024]{4,3,2,1,0:T(8,128)S(1)} %copy.77), kind=kLoop, calls=%fused_computation | loop fusion | flops 10223616 | bytes 40894464 | tf_op jit(solution)/shard_map/concatenate | solution.py:22
  804.1 12.3 %fusion = f32[2,16,1024,32]{2,3,1,0:T(8,128)} fusion(f32[2,2,16,78,1024]{4,3,2,1,0:T(8,128)S(1)} %pad_maximum_fusion, f32[32,78]{1,0:T(8,128)S(1)} %copy-done.15), kind=kOutput, calls=%fused_computation.2 | convolution fusion | flops 981467136 | bytes 14696448 | tf_op jit(solution)/shard_map/ab,czby->czay/dot_general | solution.py:98
  816.4 14.9 %bitcast_multiply_fusion = f32[2,16,32,1024]{3,2,1,0:T(8,128)} fusion(f32[2,16,32,1024]{3,2,1,0:T(8,128)S(1)} %copy-done.1, f32[2,16,1024,32]{2,3,1,0:T(8,128)} %fusion, f32[2,2,16,78,1024]{4,3,2,1,0:T(8,128)S(1)} %pad_maximum_fusion, f32[32,78]{1,0:T(8,128)S(1)} %copy-done.14), kind=kOutput, calls=%fused_computation.36 | convolution fusion | flops 984612864 | bytes 23085056 | tf_op jit(solution)/shard_map/ab,czby->czay/dot_general | solution.py:98
  (100 shorter events, 167.4 us)
Async XLA Ops:
  5.5 8.3 copy-start.18
  5.5 9.0 %copy-start.16 = (f32[2,2,31]{2,1,0:T(2,128)S(1)}, f32[2,2,31]{2,1,0:T(2,128)}, u32[]{:S(2)}) copy-start(f32[2,2,31]{2,1,0:T(2,128)} %param.7) | copy-start | bytes 1492
  5.5 37.3 %collective-permute-start = (f32[2,16,23,1024]{3,1,2,0:T(8,128)S(1)}, f32[2,16,23,1024]{3,1,2,0:T(8,128)S(1)}, u32[]{:S(2)}, u32[]{:S(2)}) collective-permute-start(f32[2,16,23,1024]{3,1,2,0:T(8,128)S(1)} %copy.101), channel_id=1, source_target_pairs={{0,8},{8,16},{16,24},{1,9},{9,17},{17,25},{2,10},{10,18},{18,26},{... | collective-permute-start | bytes 9043976 | tf_op jit(solution)/shard_map/ppermute | solution.py:20
  11.8 37.2 %collective-permute-start.1 = (f32[2,16,23,1024]{3,1,2,0:T(8,128)S(1)}, f32[2,16,23,1024]{3,1,2,0:T(8,128)S(1)}, u32[]{:S(2)}, u32[]{:S(2)}) collective-permute-start(f32[2,16,23,1024]{3,1,2,0:T(8,128)S(1)} %copy.102), channel_id=1, source_target_pairs={{8,0},{16,8},{24,16},{9,1},{17,9},{25,17},{10,2},{18,10},{26,18},{... | collective-permute-start | bytes 9043976 | tf_op jit(solution)/shard_map/ppermute | solution.py:21
  44.6 6.2 copy-start
  50.7 11.1 %copy-start.4 = (f32[2,16,23,1024]{3,2,1,0:T(8,128)}, f32[2,16,23,1024]{3,2,1,0:T(8,128)S(1)}, u32[]{:S(2)}) copy-start(f32[2,16,23,1024]{3,2,1,0:T(8,128)S(1)} %copy.64) | copy-start | bytes 9043972
  166.6 172.0 %all-to-all-start = ((f32[8,1,262144]{2,1,0:T(1,128)}), f32[8,1,262144]{2,1,0:T(1,128)}, u32[]{:S(2)}, u32[]{:S(2)}) async-start(f32[8,1,262144]{2,1,0:T(1,128)} %reshape.373), calls=%async_computation | async-start | bytes 16777216 | tf_op jit(solution)/shard_map/all_to_all | solution.py:83
  176.6 7.5 copy-start.17
  414.8 8.4 %copy-start.7 = (bf16[1,2,128,32,128]{2,4,3,1,0:T(8,128)(2,1)S(1)}, bf16[1,2,128,32,128]{2,4,3,1,0:T(8,128)(2,1)}, u32[]{:S(2)}) copy-start(bf16[1,2,128,32,128]{2,4,3,1,0:T(8,128)(2,1)} %copy.100) | copy-start | bytes 6291460
  427.3 8.4 %copy-start.6 = (bf16[1,2,128,32,128]{2,4,3,1,0:T(8,128)(2,1)S(1)}, bf16[1,2,128,32,128]{2,4,3,1,0:T(8,128)(2,1)}, u32[]{:S(2)}) copy-start(bf16[1,2,128,32,128]{2,4,3,1,0:T(8,128)(2,1)} %copy.103) | copy-start | bytes 6291460
  649.2 4.5 copy-start.2
  649.2 4.5 copy-start.13
  653.7 3.6 copy-start.12
  657.3 3.4 copy-start.11
  665.7 4.9 copy-start.10
  670.6 5.4 copy-start.3
  670.6 5.4 copy-start.9
  676.0 3.4 copy-start.8
  689.5 4.9 copy-start.5
  712.4 68.7 %collective-permute-start.2 = (f32[2,2,16,23,1024]{4,2,3,1,0:T(8,128)S(1)}, f32[2,2,16,23,1024]{4,2,3,1,0:T(8,128)S(1)}, u32[]{:S(2)}, u32[]{:S(2)}) collective-permute-start(f32[2,2,16,23,1024]{4,2,3,1,0:T(8,128)S(1)} %copy.75), channel_id=1, source_target_pairs={{0,8},{8,16},{16,24},{1,9},{9,17},{17,25},{2,10},{10,18},{18,26},{... | collective-permute-start | bytes 18087944 | tf_op jit(solution)/shard_map/ppermute | solution.py:20
  719.9 69.5 %collective-permute-start.3 = (f32[2,2,16,23,1024]{4,2,3,1,0:T(8,128)S(1)}, f32[2,2,16,23,1024]{4,2,3,1,0:T(8,128)S(1)}, u32[]{:S(2)}, u32[]{:S(2)}) collective-permute-start(f32[2,2,16,23,1024]{4,2,3,1,0:T(8,128)S(1)} %copy.76), channel_id=1, source_target_pairs={{8,0},{16,8},{24,16},{9,1},{17,9},{25,17},{10,2},{18,10},{26,18},{... | collective-permute-start | bytes 18087944 | tf_op jit(solution)/shard_map/ppermute | solution.py:21
  795.6 8.4 %copy-start.15 = (f32[32,78]{1,0:T(8,128)S(1)}, f32[32,78]{1,0:T(8,128)}, u32[]{:S(2)}) copy-start(f32[32,78]{1,0:T(8,128)} %get-tuple-element.15) | copy-start | bytes 29956
  804.0 12.3 %copy-start.1 = (f32[2,16,32,1024]{3,2,1,0:T(8,128)S(1)}, f32[2,16,32,1024]{3,2,1,0:T(8,128)}, u32[]{:S(2)}) copy-start(f32[2,16,32,1024]{3,2,1,0:T(8,128)} %param.5) | copy-start | bytes 12582916
  804.1 12.3 %copy-start.14 = (f32[32,78]{1,0:T(8,128)S(1)}, f32[32,78]{1,0:T(8,128)}, u32[]{:S(2)}) copy-start(f32[32,78]{1,0:T(8,128)} %get-tuple-element.62) | copy-start | bytes 29956
where the time goes:
time: 839 us; the launch traced here: 831 us
  waiting for transfers between devices  232 us (28%)
  local copies, waits for them, and re-layouts  201 us (24%)
  blocking collectives  187 us (22%)
  matrix products  126 us (15%)
  other arithmetic  66.6 us (8%)
  starting transfers between devices  17.9 us (2%)
    all_to_all x1, blocking collectives, shards(): lax.all_to_all(jnp.stack(spread), 'slab', split_axis=2, concat_axis=4, ti...  187 us
    all_to_all x1, waiting for transfers between devices, shards(): lax.all_to_all(jnp.stack(blurred), 'slab', split_axis=4, concat_axis=2, t...  151 us
    ppermute x2, waiting for transfers between devices, with_halo(): before = lax.ppermute(last, axis, up)  71.8 us
    unnamed x47, local copies, waits for them, and re-layouts  65 us
    dot_general x12, matrix products, blocked_rows(): jnp.einsum('czxkj,ji->czxki', padded[:, :, :, shifted:shifted + blocks],...  49.3 us
    another operation x3, local copies, waits for them, and re-layouts, shards(): jnp.stack(blurred)  36.7 us
    dot_general x2, matrix products, shards(): jnp.einsum('ab,czby->czay', across, fringe[which], precision=HIGHEST)  27.2 us
    all_to_all x1, other arithmetic, shards(): lax.all_to_all(jnp.stack(blurred), 'slab', split_axis=4, concat_axis=2, t...  26.4 us
  transfers between devices with their start and end apart: 5, of which 5 were waited for; matrix products, arithmetic and copies ran while one was open for 5% of the time, Pallas kernels for 0%

commit v1 on v0

--- a/solution.py
+++ b/solution.py
@@ -8,6 +8,17 @@
 HALO = 23
 BACKGROUND = 0.05
 HIGHEST = lax.Precision.HIGHEST
+
+
+def split_up(x, dim, devices):
+    before, after = (x.shape[:dim], x.shape[dim + 1 :])
+    return jnp.moveaxis(x.reshape(*before, devices, -1, *after), dim, 0)
+
+
+def in_order(blocks, dim):
+    dims = list(blocks.shape[1:])
+    dims[dim] *= blocks.shape[0]
+    return jnp.moveaxis(blocks, 0, dim).reshape(dims)
 
 
 def with_halo(value, sides, width):
@@ -86,7 +97,17 @@
         imaged = jnp.einsum("oi,cixy->coxy", axial[which], columns[which], precision=HIGHEST)
         quotient = recorded[which].astype(jnp.float32) / (imaged + BACKGROUND)
         spread.append(jnp.einsum("oi,coxy->cixy", axial[which], quotient, precision=HIGHEST))
-    planes = lax.all_to_all(jnp.stack(spread), "slab", split_axis=2, concat_axis=4, tiled=True)
+    x = jnp.stack(spread)
+    size, place = (lax.axis_size("slab"), lax.axis_index("slab"))
+    tiles = split_up(x, 2, size)
+    finished = [tiles[place]]
+    for step in range(1, size):
+        sent = tiles[(place + step) % size]
+        finished.append(
+            lax.ppermute(sent, "slab", [(i_2, (i_2 + step) % size) for i_2 in range(size)])
+        )
+    tiles = jnp.stack(finished)[(place - jnp.arange(size)) % size]
+    planes = in_order(tiles, 4)
     returned = [
         blocked_rows(planes[which], along_y[which], offsets[which, 1], YBLK, True)
         for which in range(views_n)

time: 839 us -> 838 us (level)
  the two profiles are of different devices: /device:TPU:1 before, /device:TPU:25 now
where the time goes in v1:
time: 838 us; the launch traced here: 831 us
  waiting for transfers between devices  283 us (34%)
  local copies, waits for them, and re-layouts  221 us (26%)
  starting transfers between devices  132 us (16%)
  matrix products  129 us (15%)
  other arithmetic  65.3 us (8%)
    all_to_all x1, waiting for transfers between devices, shards(): lax.all_to_all(jnp.stack(blurred), 'slab', split_axis=4, concat_axis=2, t...  149 us
    ppermute x7, starting transfers between devices, shards(): lax.ppermute(sent, 'slab', [(i_2, (i_2 + step) % size) for i_2 in range(s...  115 us
    unnamed x58, local copies, waits for them, and re-layouts  77.6 us
    ppermute x2, waiting for transfers between devices, with_halo(): before = lax.ppermute(last, axis, up)  71.8 us
    ppermute x7, waiting for transfers between devices, shards(): lax.ppermute(sent, 'slab', [(i_2, (i_2 + step) % size) for i_2 in range(s...  53.6 us
    dot_general x12, matrix products, blocked_rows(): jnp.einsum('czxkj,ji->czxki', padded[:, :, :, shifted:shifted + blocks],...  49.1 us
    another operation x3, local copies, waits for them, and re-layouts, shards(): jnp.stack(blurred)  36.7 us
    dot_general x2, matrix products, shards(): jnp.einsum('ab,czby->czay', across, fringe[which], precision=HIGHEST)  27.2 us
  transfers between devices with their start and end apart: 12, of which 8 were waited for; matrix products, arithmetic and copies ran while one was open for 7% of the time, Pallas kernels for 0%

profile of v1, /device:TPU:25, one launch (start us, length us, event | category | flops | bytes accessed | tf_op | source)
XLA Modules:
  0.0 830.7 jit_solution(13230410909537027715)
XLA Ops:
  29.5 12.5 %collective-permute-done = f32[2,16,23,1024]{3,1,2,0:T(8,128)S(1)} collective-permute-done((f32[2,16,23,1024]{3,1,2,0:T(8,128)S(1)}, f32[2,16,23,1024]{3,1,2,0:T(8,128)S(1)}, u32[]{:S(2)}, u32[]{:S(2)}) %collective-permute-start) | collective-permute-done | bytes 3014688 | tf_op jit(solution)/shard_map/ppermute | solution.py:31
  49.9 11.1 %fusion.3 = f32[2,16,1024,32]{2,3,1,0:T(8,128)S(1)} fusion(f32[2,16,23,1024]{3,2,1,0:T(8,128)S(1)} %copy.101, f32[2,16,32,1024]{3,2,1,0:T(8,128)S(1)} %copy-done, f32[2,16,23,1024]{3,2,1,0:T(8,128)S(1)} %copy.100, f32[32,78]{1,0:T(8,128)S(1)} %get-tuple-element.69), kind=kOutput, calls=%fused_computation.37 | convolution fusion | flops 986578944 | bytes 14427904 | tf_op jit(solution)/shard_map/ab,czby->czay/dot_general | solution.py:92
  79.1 13.7 %fusion.2 = f32[2,16,1024,32]{2,3,1,0:T(8,128)S(1)} fusion(f32[2,16,23,1024]{3,2,1,0:T(8,128)} %copy-done.4, f32[2,16,32,1024]{3,2,1,0:T(8,128)} %param.5, f32[2,16,23,1024]{3,2,1,0:T(8,128)S(1)} %copy.100, f32[32,78]{1,0:T(8,128)S(1)} %get-tuple-element.16), kind=kOutput, calls=%fused_computation.36 | convolution fusion | flops 986578944 | bytes 14427904 | tf_op jit(solution)/shard_map/ab,czby->czay/dot_general | solution.py:92
  110.4 8.3 %pad_maximum_fusion.2 = f32[2,2,16,32,1024]{4,3,2,1,0:T(8,128)} fusion(f32[1,2,16,32,1024]{4,3,2,1,0:T(8,128)} %stack_reshape.13, f32[1,2,16,32,1024]{4,3,2,1,0:T(8,128)} %stack_reshape.12), kind=kLoop, calls=%fused_computation.31 | loop fusion | flops 2097152 | bytes 16777216 | tf_op jit(solution)/shard_map/stack | solution.py:94
  118.7 26.6 %copy.102 = f32[2,2,16,32,1024]{3,2,1,0,4:T(8,128)} copy(f32[2,2,16,32,1024]{4,3,2,1,0:T(8,128)} %pad_maximum_fusion.2) | data formatting | bytes 16777216 | tf_op jit(solution)/shard_map/stack | solution.py:94
  145.3 20.5 %reshape.453 = f32[8,1,262144]{2,1,0:T(1,128)} reshape(f32[1024,2,2,16,32]{4,3,2,1,0:T(8,128)} %bitcast.226) | data formatting | bytes 16777216
  187.0 149.0 %all-to-all-done = f32[8,1,262144]{2,1,0:T(1,128)} async-done(((f32[8,1,262144]{2,1,0:T(1,128)}), f32[8,1,262144]{2,1,0:T(1,128)}, u32[]{:S(2)}, u32[]{:S(2)}) %all-to-all-start) | async-done | bytes 8388640 | tf_op jit(solution)/shard_map/all_to_all | solution.py:94
  336.4 26.4 %reduce.6 = f32[8,262144]{1,0:T(8,128)} reduce(f32[8,1,262144]{2,1,0:T(1,128)} %all-to-all-done, f32[]{:T(128)} %broadcast.461), dimensions={1}, to_apply=%all_to_all.11.reduce_sub_computation | reduce | bytes 16777220 | tf_op jit(solution)/shard_map/all_to_all | solution.py:94
  362.8 25.3 %reshape.454 = f32[1024,2,2,16,32]{4,3,2,1,0:T(8,128)} reshape(f32[8,262144]{1,0:T(8,128)} %reduce.6) | data formatting | bytes 16777216
  388.1 18.4 %copy.148 = f32[2,2,16,32,8,128]{5,4,3,2,1,0:T(8,128)} copy(f32[2,2,16,32,8,128]{3,2,1,0,5,4:T(8,128)} %bitcast.227) | data formatting | bytes 16777216 | tf_op jit(solution)/shard_map/all_to_all | solution.py:94
  412.1 8.8 %fusion.16 = f32[2,32,128,128]{3,2,1,0:T(8,128)S(1)} fusion(f32[2,128,32,128]{3,2,1,0:T(8,128)S(1)} %bitcast.239, f32[128,128]{1,0:T(8,128)S(1)} %get-tuple-element.5), kind=kOutput, calls=%fused_computation.55 | convolution fusion | flops 1610612736 | bytes 8454144 | tf_op jit(solution)/shard_map/oi,cixy->coxy/dot_general | solution.py:97
  425.9 9.0 %fusion.18 = f32[2,32,128,128]{3,2,1,0:T(8,128)S(1)} fusion(f32[2,128,32,128]{3,2,1,0:T(8,128)S(1)} %bitcast.238, f32[128,128]{1,0:T(8,128)S(1)} %get-tuple-element.6), kind=kOutput, calls=%fused_computation.57 | convolution fusion | flops 1610612736 | bytes 8454144 | tf_op jit(solution)/shard_map/oi,cixy->coxy/dot_general | solution.py:97
  456.0 13.4 %collective-permute-done.2 = f32[2,2,16,32,128]{4,3,2,1,0:T(8,128)} collective-permute-done((f32[2,2,16,32,128]{4,3,2,1,0:T(8,128)}, f32[2,2,16,32,128]{4,3,2,1,0:T(8,128)}, u32[]{:S(2)}, u32[]{:S(2)}) %collective-permute-start.2) | collective-permute-done | bytes 1048608 | tf_op jit(solution)/shard_map/ppermute | solution.py:107
  471.6 109.7 %collective-permute-start.8 = (f32[2,2,16,32,128]{4,3,2,1,0:T(8,128)S(1)}, f32[2,2,16,32,128]{4,3,2,1,0:T(8,128)S(1)}, u32[]{:S(2)}, u32[]{:S(2)}) collective-permute-start(f32[2,2,16,32,128]{4,3,2,1,0:T(8,128)S(1)} %bitcast.247), channel_id=1, source_target_pairs={{0,7},{1,0},{2,1},{3,2},{4,3},{5,4},{6,5},{7,6},{8,15},{9,8},{10,9... | collective-permute-start | bytes 3145736 | tf_op jit(solution)/shard_map/ppermute | solution.py:107
  583.6 19.5 %collective-permute-done.4 = f32[2,2,16,32,128]{4,3,2,1,0:T(8,128)} collective-permute-done((f32[2,2,16,32,128]{4,3,2,1,0:T(8,128)}, f32[2,2,16,32,128]{4,3,2,1,0:T(8,128)}, u32[]{:S(2)}, u32[]{:S(2)}) %collective-permute-start.4) | collective-permute-done | bytes 1048608 | tf_op jit(solution)/shard_map/ppermute | solution.py:107
  605.3 20.7 %collective-permute-done.5 = f32[2,2,16,32,128]{4,3,2,1,0:T(8,128)S(1)} collective-permute-done((f32[2,2,16,32,128]{4,3,2,1,0:T(8,128)S(1)}, f32[2,2,16,32,128]{4,3,2,1,0:T(8,128)S(1)}, u32[]{:S(2)}, u32[]{:S(2)}) %collective-permute-start.5) | collective-permute-done | bytes 1048608 | tf_op jit(solution)/shard_map/ppermute | solution.py:107
  630.3 7.7 gather_fusion
  638.0 11.5 %copy.170 = f32[8,2,2,16,32,128]{5,0,4,3,2,1:T(8,128)S(1)} copy(f32[8,2,2,16,32,128]{5,4,3,2,1,0:T(8,128)} %gather_fusion) | data formatting | bytes 16777216 | tf_op jit(solution)/shard_map/gather | solution.py:109
  696.9 9.5 %fusion.76 = (f32[2,2,16,23,1024]{4,3,2,1,0:T(8,128)}, f32[2,2,16,23,1024]{4,3,2,1,0:T(8,128)S(1)}) fusion(f32[2,2,16,32,1024]{4,3,2,1,0:T(8,128)} %constant_dynamic-update-slice_fusion), kind=kLoop, calls=%fused_computation.209 | loop fusion | bytes 24117248 | tf_op jit(solution)/shard_map/slice | solution.py:29
  706.4 6.3 copy.122
  721.5 59.3 %collective-permute-done.9 = f32[2,2,16,23,1024]{4,2,3,1,0:T(8,128)S(1)} collective-permute-done((f32[2,2,16,23,1024]{4,2,3,1,0:T(8,128)S(1)}, f32[2,2,16,23,1024]{4,2,3,1,0:T(8,128)S(1)}, u32[]{:S(2)}, u32[]{:S(2)}) %collective-permute-start.9) | collective-permute-done | bytes 6029344 | tf_op jit(solution)/shard_map/ppermute | solution.py:31
  794.8 8.4 %pad_maximum_fusion = f32[2,2,16,78,1024]{4,3,2,1,0:T(8,128)S(1)} fusion(f32[2,2,16,23,1024]{4,3,2,1,0:T(8,128)} %copy.125, f32[2,2,16,32,1024]{4,3,2,1,0:T(8,128)} %constant_dynamic-update-slice_fusion, f32[2,2,16,23,1024]{4,3,2,1,0:T(8,128)S(1)} %copy.124), kind=kLoop, calls=%fused_computation.1 | loop fusion | flops 10223616 | bytes 40894464 | tf_op jit(solution)/shard_map/concatenate | solution.py:33
  803.3 12.3 %fusion = f32[2,16,1024,32]{2,3,1,0:T(8,128)} fusion(f32[2,2,16,78,1024]{4,3,2,1,0:T(8,128)S(1)} %pad_maximum_fusion, f32[32,78]{1,0:T(8,128)S(1)} %copy-done.17), kind=kOutput, calls=%fused_computation.19 | convolution fusion | flops 981467136 | bytes 14696448 | tf_op jit(solution)/shard_map/ab,czby->czay/dot_general | solution.py:119
  815.6 14.9 %bitcast_multiply_fusion = f32[2,16,32,1024]{3,2,1,0:T(8,128)} fusion(f32[2,16,32,1024]{3,2,1,0:T(8,128)S(1)} %copy-done.1, f32[2,16,1024,32]{2,3,1,0:T(8,128)} %fusion, f32[2,2,16,78,1024]{4,3,2,1,0:T(8,128)S(1)} %pad_maximum_fusion, f32[32,78]{1,0:T(8,128)S(1)} %copy-done.16), kind=kOutput, calls=%fused_computation.52 | convolution fusion | flops 984612864 | bytes 23085056 | tf_op jit(solution)/shard_map/ab,czby->czay/dot_general | solution.py:119
  (135 shorter events, 207.4 us)
Async XLA Ops:
  5.5 7.5 copy-start.20
  5.5 8.1 copy-start.18
  5.5 36.5 %collective-permute-start = (f32[2,16,23,1024]{3,1,2,0:T(8,128)S(1)}, f32[2,16,23,1024]{3,1,2,0:T(8,128)S(1)}, u32[]{:S(2)}, u32[]{:S(2)}) collective-permute-start(f32[2,16,23,1024]{3,1,2,0:T(8,128)S(1)} %copy.152), channel_id=1, source_target_pairs={{0,8},{8,16},{16,24},{1,9},{9,17},{17,25},{2,10},{10,18},{18,26},{... | collective-permute-start | bytes 9043976 | tf_op jit(solution)/shard_map/ppermute | solution.py:31
  10.9 37.2 %collective-permute-start.1 = (f32[2,16,23,1024]{3,1,2,0:T(8,128)S(1)}, f32[2,16,23,1024]{3,1,2,0:T(8,128)S(1)}, u32[]{:S(2)}, u32[]{:S(2)}) collective-permute-start(f32[2,16,23,1024]{3,1,2,0:T(8,128)S(1)} %copy.153), channel_id=1, source_target_pairs={{8,0},{16,8},{24,16},{9,1},{17,9},{25,17},{10,2},{18,10},{26,18},{... | collective-permute-start | bytes 9043976 | tf_op jit(solution)/shard_map/ppermute | solution.py:32
  43.7 6.2 copy-start
  49.9 11.1 %copy-start.4 = (f32[2,16,23,1024]{3,2,1,0:T(8,128)}, f32[2,16,23,1024]{3,2,1,0:T(8,128)S(1)}, u32[]{:S(2)}) copy-start(f32[2,16,23,1024]{3,2,1,0:T(8,128)S(1)} %copy.101) | copy-start | bytes 9043972
  165.8 170.2 %all-to-all-start = ((f32[8,1,262144]{2,1,0:T(1,128)}), f32[8,1,262144]{2,1,0:T(1,128)}, u32[]{:S(2)}, u32[]{:S(2)}) async-start(f32[8,1,262144]{2,1,0:T(1,128)} %reshape.453), calls=%async_computation | async-start | bytes 16777216 | tf_op jit(solution)/shard_map/all_to_all | solution.py:94
  175.7 7.5 copy-start.19
  412.1 8.8 %copy-start.9 = (bf16[1,2,128,32,128]{2,4,3,1,0:T(8,128)(2,1)S(1)}, bf16[1,2,128,32,128]{2,4,3,1,0:T(8,128)(2,1)}, u32[]{:S(2)}) copy-start(bf16[1,2,128,32,128]{2,4,3,1,0:T(8,128)(2,1)} %copy.154) | copy-start | bytes 6291460
  425.9 13.9 %copy-start.6 = (f32[2,32,128,128]{2,3,1,0:T(8,128)}, f32[2,32,128,128]{2,3,1,0:T(8,128)S(1)}, u32[]{:S(2)}) copy-start(f32[2,32,128,128]{2,3,1,0:T(8,128)S(1)} %fusion.12) | copy-start | bytes 12582916
  425.9 9.0 %copy-start.8 = (bf16[1,2,128,32,128]{2,4,3,1,0:T(8,128)(2,1)S(1)}, bf16[1,2,128,32,128]{2,4,3,1,0:T(8,128)(2,1)}, u32[]{:S(2)}) copy-start(bf16[1,2,128,32,128]{2,4,3,1,0:T(8,128)(2,1)} %copy.151) | copy-start | bytes 6291460
  443.2 26.2 %collective-permute-start.2 = (f32[2,2,16,32,128]{4,3,2,1,0:T(8,128)}, f32[2,2,16,32,128]{4,3,2,1,0:T(8,128)}, u32[]{:S(2)}, u32[]{:S(2)}) collective-permute-start(f32[2,2,16,32,128]{4,3,2,1,0:T(8,128)} %bitcast.225), channel_id=1, source_target_pairs={{0,1},{1,2},{2,3},{3,4},{4,5},{5,6},{6,7},{7,0},{8,9},{9,10},{10,1... | collective-permute-start | bytes 3145736 | tf_op jit(solution)/shard_map/ppermute | solution.py:107
  445.0 26.6 %collective-permute-start.3 = (f32[2,2,16,32,128]{4,3,2,1,0:T(8,128)}, f32[2,2,16,32,128]{4,3,2,1,0:T(8,128)}, u32[]{:S(2)}, u32[]{:S(2)}) collective-permute-start(f32[2,2,16,32,128]{4,3,2,1,0:T(8,128)} %bitcast.224), channel_id=1, source_target_pairs={{0,2},{1,3},{2,4},{3,5},{4,6},{5,7},{6,0},{7,1},{8,10},{9,11},{10,... | collective-permute-start | bytes 3145736 | tf_op jit(solution)/shard_map/ppermute | solution.py:107
  448.2 154.8 %collective-permute-start.4 = (f32[2,2,16,32,128]{4,3,2,1,0:T(8,128)}, f32[2,2,16,32,128]{4,3,2,1,0:T(8,128)}, u32[]{:S(2)}, u32[]{:S(2)}) collective-permute-start(f32[2,2,16,32,128]{4,3,2,1,0:T(8,128)} %bitcast.223), channel_id=1, source_target_pairs={{0,3},{1,4},{2,5},{3,6},{4,7},{5,0},{6,1},{7,2},{8,11},{9,12},{10,... | collective-permute-start | bytes 3145736 | tf_op jit(solution)/shard_map/ppermute | solution.py:107
  450.4 176.7 %collective-permute-start.6 = (f32[2,2,16,32,128]{4,3,2,1,0:T(8,128)S(1)}, f32[2,2,16,32,128]{4,3,2,1,0:T(8,128)S(1)}, u32[]{:S(2)}, u32[]{:S(2)}) collective-permute-start(f32[2,2,16,32,128]{4,3,2,1,0:T(8,128)S(1)} %bitcast.246), channel_id=1, source_target_pairs={{0,5},{1,6},{2,7},{3,0},{4,1},{5,2},{6,3},{7,4},{8,13},{9,14},{10,... | collective-permute-start | bytes 3145736 | tf_op jit(solution)/shard_map/ppermute | solution.py:107
  453.9 172.2 %collective-permute-start.5 = (f32[2,2,16,32,128]{4,3,2,1,0:T(8,128)S(1)}, f32[2,2,16,32,128]{4,3,2,1,0:T(8,128)S(1)}, u32[]{:S(2)}, u32[]{:S(2)}) collective-permute-start(f32[2,2,16,32,128]{4,3,2,1,0:T(8,128)S(1)} %bitcast.249), channel_id=1, source_target_pairs={{0,4},{1,5},{2,6},{3,7},{4,0},{5,1},{6,2},{7,3},{8,12},{9,13},{10,... | collective-permute-start | bytes 3145736 | tf_op jit(solution)/shard_map/ppermute | solution.py:107
  469.3 158.9 %collective-permute-start.7 = (f32[2,2,16,32,128]{4,3,2,1,0:T(8,128)S(1)}, f32[2,2,16,32,128]{4,3,2,1,0:T(8,128)S(1)}, u32[]{:S(2)}, u32[]{:S(2)}) collective-permute-start(f32[2,2,16,32,128]{4,3,2,1,0:T(8,128)S(1)} %bitcast.248), channel_id=1, source_target_pairs={{0,6},{1,7},{2,0},{3,1},{4,2},{5,3},{6,4},{7,5},{8,14},{9,15},{10,... | collective-permute-start | bytes 3145736 | tf_op jit(solution)/shard_map/ppermute | solution.py:107
  471.6 157.6 %collective-permute-start.8 = (f32[2,2,16,32,128]{4,3,2,1,0:T(8,128)S(1)}, f32[2,2,16,32,128]{4,3,2,1,0:T(8,128)S(1)}, u32[]{:S(2)}, u32[]{:S(2)}) collective-permute-start(f32[2,2,16,32,128]{4,3,2,1,0:T(8,128)S(1)} %bitcast.247), channel_id=1, source_target_pairs={{0,7},{1,0},{2,1},{3,2},{4,3},{5,4},{6,5},{7,6},{8,15},{9,8},{10,9... | collective-permute-start | bytes 3145736 | tf_op jit(solution)/shard_map/ppermute | solution.py:107
  670.9 5.4 copy-start.11
  712.7 68.0 %collective-permute-start.9 = (f32[2,2,16,23,1024]{4,2,3,1,0:T(8,128)S(1)}, f32[2,2,16,23,1024]{4,2,3,1,0:T(8,128)S(1)}, u32[]{:S(2)}, u32[]{:S(2)}) collective-permute-start(f32[2,2,16,23,1024]{4,2,3,1,0:T(8,128)S(1)} %copy.122), channel_id=1, source_target_pairs={{0,8},{8,16},{16,24},{1,9},{9,17},{17,25},{2,10},{10,18},{18,26},{... | collective-permute-start | bytes 18087944 | tf_op jit(solution)/shard_map/ppermute | solution.py:31
  719.1 69.5 %collective-permute-start.10 = (f32[2,2,16,23,1024]{4,2,3,1,0:T(8,128)S(1)}, f32[2,2,16,23,1024]{4,2,3,1,0:T(8,128)S(1)}, u32[]{:S(2)}, u32[]{:S(2)}) collective-permute-start(f32[2,2,16,23,1024]{4,2,3,1,0:T(8,128)S(1)} %copy.123), channel_id=1, source_target_pairs={{8,0},{16,8},{24,16},{9,1},{17,9},{25,17},{10,2},{18,10},{26,18},{... | collective-permute-start | bytes 18087944 | tf_op jit(solution)/shard_map/ppermute | solution.py:32
  794.8 8.4 %copy-start.17 = (f32[32,78]{1,0:T(8,128)S(1)}, f32[32,78]{1,0:T(8,128)}, u32[]{:S(2)}) copy-start(f32[32,78]{1,0:T(8,128)} %get-tuple-element.15) | copy-start | bytes 29956
  803.3 12.3 %copy-start.1 = (f32[2,16,32,1024]{3,2,1,0:T(8,128)S(1)}, f32[2,16,32,1024]{3,2,1,0:T(8,128)}, u32[]{:S(2)}) copy-start(f32[2,16,32,1024]{3,2,1,0:T(8,128)} %param.5) | copy-start | bytes 12582916
  803.3 12.3 %copy-start.16 = (f32[32,78]{1,0:T(8,128)S(1)}, f32[32,78]{1,0:T(8,128)}, u32[]{:S(2)}) copy-start(f32[32,78]{1,0:T(8,128)} %get-tuple-element.70) | copy-start | bytes 29956
  (9 other events, 36.6 us)
